TPU v7x, 32 devices: a whole 2x2x4 slice. The times are simulated.
32 devices in a mesh: tower: 2 (over y), dp: 16 (over z, x, core).
Axes of the slice: x: 2, y: 2, z: 4, core: 2. Of those that a mesh axis runs over, the one named last changes fastest.
Arguments:
- tokens: bfloat16 [2, 4096, 768], P('tower', 'dp'), may hold values from -6 to 6
- query_lengths: int32 [64], P('dp'), may hold values from 8 to 64, as said below
- doc_lengths: int32 [16], P('dp'), may hold values from 32 to 256, as said below
- positives: int32 [64], replicated, may hold values from 0 to 15
- w_qkv: bfloat16 [768, 2304], P('dp'), may hold values from -0.21875 to 0.21875
- w_out: bfloat16 [768, 768], P('dp'), may hold values from -0.21875 to 0.21875
- w_gate: bfloat16 [768, 3072], P('dp'), may hold values from -0.21875 to 0.21875
- w_up: bfloat16 [768, 3072], P('dp'), may hold values from -0.21875 to 0.21875
- w_down: bfloat16 [3072, 768], P('dp'), may hold values from -0.109375 to 0.109375
- ln1_gain: bfloat16 [768], P('dp'), may hold values from 0.5 to 1.5
- first_layernorm_shift: bfloat16 [768], P('dp'), may hold values from -0.59765625 to 0.59765625
- ln2_gain: bfloat16 [768], P('dp'), may hold values from 0.5 to 1.5
- ln2_bias: bfloat16 [768], P('dp'), may hold values from -0.6 to 0.6
Outputs:
- loss: float32 [], replicated
- query_embeddings: float32 [64, 768], P('dp')
- doc_embeddings: float32 [16, 768], P('dp')
- token_grad: float32 [2, 4096, 768], P('tower', 'dp')
- w_qkv_grad: float32 [768, 2304], P('dp')
- w_out_grad: float32 [768, 768], P('dp')
- w_gate_grad: float32 [768, 3072], P('dp')
- w_up_grad: float32 [768, 3072], P('dp')
- w_down_grad: float32 [3072, 768], P('dp')
- ln1_gain_grad: float32 [768], P('dp')
- ln1_bias_grad: float32 [768], P('dp')
- ln2_gain_grad: float32 [768], P('dp')
- ln2_bias_grad: float32 [768], P('dp')
Inputs may be any that keep to these rules, and one draw needn't show every extreme that they name: `query_lengths`: each query has 8 to 64 real tokens in the first slots of its block; some query has 64. `doc_lengths`: each document has 32 to 256 real tokens in the first slots; some document has 256.
All inputs are finite; a program needn't handle non-finite values.
Results may differ from a plain program's by a relative error of at most 0.0085.
Values may be sent and summed in bfloat16 or wider, within the bound.
A program may use at most 128 MiB of HBM per device.

v0:
```python
import jax
import jax.numpy as jnp
from jax import lax
from jax.sharding import PartitionSpec as P

D = 768
HEADS = 12
HEAD = 64
QLEN = 64
QPD = 4
exact_product_accuracy = lax.Precision.HIGHEST
rope_base = 1000.0
contrast_sharpness_factor = 0.02


def product(left, right):
    return jnp.dot(left, right, preferred_element_type=jnp.float32)


def rotary_tables(places):
    freqs = jnp.power(rope_base, -2.0 * jnp.arange(HEAD // 2).astype(jnp.float32) / HEAD)
    angles = places[:, None] * freqs[None, :]
    return (jnp.cos(angles)[:, None, :], jnp.sin(angles)[:, None, :])


def rotate(values, cosines, sines):
    half_dim = values.shape[-1] // 2
    first = values[..., :half_dim]
    second = values[..., half_dim:]
    return jnp.concatenate(
        [first * cosines - second * sines, second * cosines + first * sines], axis=-1
    )


def layer_norm(hidden, gain, offset):
    average = jnp.mean(hidden, -1, keepdims=True)
    centred = hidden - average
    variance = jnp.mean(centred * centred, -1, keepdims=True)
    return centred * lax.rsqrt(variance + 1e-05) * gain + offset


def normalize(pooled):
    return pooled * lax.rsqrt(jnp.sum(pooled * pooled, -1, keepdims=True) + 1e-06)


def layout(tower_id, query_len, doc_len, count):
    places = jnp.arange(count)
    span = jnp.where(tower_id == 0, QLEN, count)
    segment = places // span
    offset_in = places - segment * span
    slots = jnp.arange(QPD)
    seg_limit = jnp.where(tower_id == 0, query_len, doc_len[0] * jnp.ones_like(query_len))
    limit = jnp.sum(jnp.where(segment[:, None] == slots[None, :], seg_limit[None, :], 0), axis=1)
    valid = offset_in < limit
    allowed = (segment[:, None] == segment[None, :]) & valid[None, :]
    member = (segment[None, :] == slots[:, None]) & valid[None, :]
    pool_matrix = jnp.where(member, 1.0 / seg_limit[:, None].astype(jnp.float32), 0.0)
    return (offset_in.astype(jnp.float32), allowed, pool_matrix)


def swish_product(left, right):
    return jax.nn.silu(left) * right


def on_device(
    tokens,
    query_lengths,
    doc_lengths,
    positives,
    w_qkv,
    w_out,
    w_gate,
    w_up,
    w_down,
    ln1_gain,
    first_layernorm_shift,
    ln2_gain,
    ln2_bias,
):
    tower_id = lax.axis_index("tower")
    device_id = lax.axis_index("dp")
    groups = lax.axis_size("dp")
    full = (
        lax.all_gather(w_qkv, "dp", axis=0, tiled=True),
        lax.all_gather(w_out, "dp", axis=0, tiled=True),
        lax.all_gather(w_gate, "dp", axis=0, tiled=True),
        lax.all_gather(w_up, "dp", axis=0, tiled=True),
        lax.all_gather(w_down, "dp", axis=0, tiled=True),
        lax.all_gather(ln1_gain, "dp", axis=0, tiled=True),
        lax.all_gather(first_layernorm_shift, "dp", axis=0, tiled=True),
        lax.all_gather(ln2_gain, "dp", axis=0, tiled=True),
        lax.all_gather(ln2_bias, "dp", axis=0, tiled=True),
    )
    qkv_full, out_full, gate_full, up_full, down_full = (
        full[0],
        full[1],
        full[2],
        full[3],
        full[4],
    )
    gain_one = full[5].astype(jnp.float32)
    bias_one = full[6].astype(jnp.float32)
    gain_two = full[7].astype(jnp.float32)
    bias_two = full[8].astype(jnp.float32)
    inputs = tokens[0]
    count = inputs.shape[0]
    places, allowed, pool_matrix = layout(tower_id, query_lengths, doc_lengths, count)
    cosines, sines = rotary_tables(places)
    packed = product(inputs, qkv_full)
    raw_query = packed[:, :D].reshape(count, HEADS, HEAD)
    raw_key = packed[:, D : 2 * D].reshape(count, HEADS, HEAD)

    def rotate_both(first, second):
        return (rotate(first, cosines, sines), rotate(second, cosines, sines))

    rotated, rotary_back = jax.vjp(rotate_both, raw_query, raw_key)
    query_low = rotated[0].astype(jnp.bfloat16)
    key_low = rotated[1].astype(jnp.bfloat16)
    value_low = packed[:, 2 * D :].reshape(count, HEADS, HEAD).astype(jnp.bfloat16)
    scale = HEAD ** (-0.5)

    def masked_scores():
        scores = (
            jnp.einsum("ihd,jhd->hij", query_low, key_low, preferred_element_type=jnp.float32)
            * scale
        )
        return jnp.where(allowed[None], scores, -1e30)

    scores = masked_scores()
    peak = jnp.max(scores, -1, keepdims=True)
    log_total = peak + jnp.log(jnp.sum(jnp.exp(scores - peak), -1, keepdims=True))
    probs_low = jnp.exp(scores - log_total).astype(jnp.bfloat16)
    mixed = jnp.einsum("hij,jhd->ihd", probs_low, value_low, preferred_element_type=jnp.float32)
    mixed_low = mixed.reshape(count, D).astype(jnp.bfloat16)
    attended = product(mixed_low, out_full)
    inputs_wide = inputs.astype(jnp.float32)
    normed_one, norm_one_back = jax.vjp(layer_norm, inputs_wide + attended, gain_one, bias_one)
    feed = normed_one.astype(jnp.bfloat16)
    gate = product(feed, gate_full)
    up_part = product(feed, up_full)
    hidden_wide, swish_back = jax.vjp(swish_product, gate, up_part)
    hidden = hidden_wide.astype(jnp.bfloat16)
    branch = product(hidden, down_full)
    normed_two, norm_two_back = jax.vjp(layer_norm, normed_one + branch, gain_two, bias_two)
    pooled = jnp.dot(pool_matrix, normed_two, precision=exact_product_accuracy)
    embedded, normal_back = jax.vjp(normalize, pooled)
    gathered = lax.all_gather(embedded, ("tower", "dp"), axis=0, tiled=True)
    queries_total = groups * QPD
    gathered_query_rows = gathered[:queries_total]
    gathered_document_rows = gathered[queries_total:].reshape(groups, QPD, D)[:, 0]
    pairwise_affinity_matrix = (
        jnp.dot(gathered_query_rows, gathered_document_rows.T, precision=exact_product_accuracy)
        / contrast_sharpness_factor
    )
    peak_logit = jnp.max(pairwise_affinity_matrix, -1, keepdims=True)
    log_partition_norm = peak_logit + jnp.log(
        jnp.sum(jnp.exp(pairwise_affinity_matrix - peak_logit), -1, keepdims=True)
    )
    columns = lax.broadcasted_iota(jnp.int32, pairwise_affinity_matrix.shape, 1)
    matching_labels = columns == positives[:, None]
    picked = jnp.sum(jnp.where(matching_labels, pairwise_affinity_matrix, 0.0), -1, keepdims=True)
    total = jnp.sum(log_partition_norm - picked)
    loss = total / queries_total
    similarity_gradient = (
        jnp.exp(pairwise_affinity_matrix - log_partition_norm) - matching_labels.astype(jnp.float32)
    ) / contrast_sharpness_factor
    own_rows = lax.dynamic_slice_in_dim(similarity_gradient, device_id * QPD, QPD, 0)
    query_side = jnp.dot(own_rows, gathered_document_rows, precision=exact_product_accuracy)
    own_column = lax.dynamic_slice_in_dim(similarity_gradient, device_id, 1, 1)
    doc_side = jnp.dot(own_column.T, gathered_query_rows, precision=exact_product_accuracy)
    doc_side = jnp.concatenate([doc_side, jnp.zeros((QPD - 1, D), jnp.float32)], 0)
    embed_grad = jnp.where(tower_id == 0, query_side, doc_side)
    pooled_grad = normal_back(embed_grad)[0]
    top_grad = jnp.dot(pool_matrix.T, pooled_grad, precision=exact_product_accuracy)
    sum_two, gain_two_grad, bias_two_grad = norm_two_back(top_grad)
    attention_input_cotangent, out_back, gate_back, up_back, down_back = (
        qkv_full,
        out_full,
        gate_full,
        up_full,
        down_full,
    )
    branch_low = sum_two.astype(jnp.bfloat16)
    down_grad = product(hidden.T, branch_low)
    hidden_grad = product(branch_low, down_back.T)
    gate_grad_wide, up_grad_wide = swish_back(hidden_grad)
    gate_low = gate_grad_wide.astype(jnp.bfloat16)
    up_low = up_grad_wide.astype(jnp.bfloat16)
    gate_weight_grad = product(feed.T, gate_low)
    up_weight_grad = product(feed.T, up_low)
    feed_grad = sum_two + product(gate_low, gate_back.T) + product(up_low, up_back.T)
    sum_one, gain_one_grad, bias_one_grad = norm_one_back(feed_grad)
    attend_low = sum_one.astype(jnp.bfloat16)
    out_grad = product(mixed_low.T, attend_low)
    mixed_grad = product(attend_low, out_back.T).astype(jnp.bfloat16).reshape(count, HEADS, HEAD)
    probs_again = jnp.exp(masked_scores() - log_total)
    prob_grad = jnp.einsum(
        "ihd,jhd->hij", mixed_grad, value_low, preferred_element_type=jnp.float32
    )
    score_grad = probs_again * (prob_grad - jnp.sum(probs_again * prob_grad, -1, keepdims=True))
    score_low = score_grad.astype(jnp.bfloat16)
    query_grad = (
        jnp.einsum("hij,jhd->ihd", score_low, key_low, preferred_element_type=jnp.float32) * scale
    )
    key_grad = (
        jnp.einsum("hij,ihd->jhd", score_low, query_low, preferred_element_type=jnp.float32) * scale
    )
    value_grad = jnp.einsum(
        "hij,ihd->jhd",
        probs_again.astype(jnp.bfloat16),
        mixed_grad,
        preferred_element_type=jnp.float32,
    )
    raw_query_grad, raw_key_grad = rotary_back((query_grad, key_grad))
    packed_grad = jnp.concatenate(
        [
            raw_query_grad.reshape(count, D),
            raw_key_grad.reshape(count, D),
            value_grad.reshape(count, D),
        ],
        1,
    ).astype(jnp.bfloat16)
    qkv_grad = product(inputs.T, packed_grad)
    input_grad = sum_one + product(packed_grad, attention_input_cotangent.T)
    gradients = (
        qkv_grad,
        out_grad,
        gate_weight_grad,
        up_weight_grad,
        down_grad,
        gain_one_grad,
        bias_one_grad,
        gain_two_grad,
        bias_two_grad,
    )
    partial_sums = (
        lax.psum_scatter(gradients[0], "dp", scatter_dimension=0, tiled=True),
        lax.psum_scatter(gradients[1], "dp", scatter_dimension=0, tiled=True),
        lax.psum_scatter(gradients[2], "dp", scatter_dimension=0, tiled=True),
        lax.psum_scatter(gradients[3], "dp", scatter_dimension=0, tiled=True),
        lax.psum_scatter(gradients[4], "dp", scatter_dimension=0, tiled=True),
        lax.psum_scatter(gradients[5], "dp", scatter_dimension=0, tiled=True),
        lax.psum_scatter(gradients[6], "dp", scatter_dimension=0, tiled=True),
        lax.psum_scatter(gradients[7], "dp", scatter_dimension=0, tiled=True),
        lax.psum_scatter(gradients[8], "dp", scatter_dimension=0, tiled=True),
    )
    tower_halves = (
        lax.psum_scatter(
            partial_sums[0].astype(jnp.bfloat16), "tower", scatter_dimension=0, tiled=True
        ).astype(jnp.float32),
        lax.psum_scatter(
            partial_sums[1].astype(jnp.bfloat16), "tower", scatter_dimension=0, tiled=True
        ).astype(jnp.float32),
        lax.psum_scatter(
            partial_sums[2].astype(jnp.bfloat16), "tower", scatter_dimension=0, tiled=True
        ).astype(jnp.float32),
        lax.psum_scatter(
            partial_sums[3].astype(jnp.bfloat16), "tower", scatter_dimension=0, tiled=True
        ).astype(jnp.float32),
        lax.psum_scatter(
            partial_sums[4].astype(jnp.bfloat16), "tower", scatter_dimension=0, tiled=True
        ).astype(jnp.float32),
        lax.psum_scatter(
            partial_sums[5].astype(jnp.bfloat16), "tower", scatter_dimension=0, tiled=True
        ).astype(jnp.float32),
        lax.psum_scatter(
            partial_sums[6].astype(jnp.bfloat16), "tower", scatter_dimension=0, tiled=True
        ).astype(jnp.float32),
        lax.psum_scatter(
            partial_sums[7].astype(jnp.bfloat16), "tower", scatter_dimension=0, tiled=True
        ).astype(jnp.float32),
        lax.psum_scatter(
            partial_sums[8].astype(jnp.bfloat16), "tower", scatter_dimension=0, tiled=True
        ).astype(jnp.float32),
    )
    shares = (
        lax.all_gather(tower_halves[0].astype(jnp.bfloat16), "tower", axis=0, tiled=True).astype(
            jnp.float32
        ),
        lax.all_gather(tower_halves[1].astype(jnp.bfloat16), "tower", axis=0, tiled=True).astype(
            jnp.float32
        ),
        lax.all_gather(tower_halves[2].astype(jnp.bfloat16), "tower", axis=0, tiled=True).astype(
            jnp.float32
        ),
        lax.all_gather(tower_halves[3].astype(jnp.bfloat16), "tower", axis=0, tiled=True).astype(
            jnp.float32
        ),
        lax.all_gather(tower_halves[4].astype(jnp.bfloat16), "tower", axis=0, tiled=True).astype(
            jnp.float32
        ),
        lax.all_gather(tower_halves[5].astype(jnp.bfloat16), "tower", axis=0, tiled=True).astype(
            jnp.float32
        ),
        lax.all_gather(tower_halves[6].astype(jnp.bfloat16), "tower", axis=0, tiled=True).astype(
            jnp.float32
        ),
        lax.all_gather(tower_halves[7].astype(jnp.bfloat16), "tower", axis=0, tiled=True).astype(
            jnp.float32
        ),
        lax.all_gather(tower_halves[8].astype(jnp.bfloat16), "tower", axis=0, tiled=True).astype(
            jnp.float32
        ),
    )
    query_rows = lax.dynamic_slice_in_dim(gathered_query_rows, device_id * QPD, QPD, 0)
    doc_row = lax.dynamic_slice_in_dim(gathered_document_rows, device_id, 1, 0)
    return (loss, query_rows, doc_row, input_grad[None]) + tuple(shares)


def solution(mesh):
    return jax.shard_map(
        on_device,
        mesh=mesh,
        in_specs=(
            P("tower", "dp", None),
            P("dp"),
            P("dp"),
            P(),
            P("dp", None),
            P("dp", None),
            P("dp", None),
            P("dp", None),
            P("dp", None),
            P("dp"),
            P("dp"),
            P("dp"),
            P("dp"),
        ),
        out_specs=(
            P(),
            P("dp", None),
            P("dp", None),
            P("tower", "dp", None),
            P("dp", None),
            P("dp", None),
            P("dp", None),
            P("dp", None),
            P("dp", None),
            P("dp"),
            P("dp"),
            P("dp"),
            P("dp"),
        ),
        check_vma=False,
    )
```

profile of v0, /device:TPU:0, one launch (start us, length us, event | category | flops | bytes accessed | tf_op | source)
XLA Modules:
  0.0 923.1 jit_solution(9459486310065083493)
XLA Ops:
  16.6 35.8 %all-reduce.22 = (bf16[768]{0:T(1024)(128)(2,1)S(1)}, bf16[768]{0:T(1024)(128)(2,1)S(1)}, bf16[768]{0:T(1024)(128)(2,1)S(1)}, bf16[768]{0:T(1024)(128)(2,1)S(1)}) all-reduce(bf16[768]{0:T(1024)(128)(2,1)S(1)} %dynamic-update-slice.1, bf16[768]{0:T(1024)(128)(2,1)S(1)} %dynamic-update-slice, ...), channel_id=1, replica_groups=mesh['tower'=2,'dp'=16] {'dp'}, use_global_device_ids=true, to_apply=%add.6 | all-reduce | flops 3072 | bytes 12288
  71.6 28.5 %all-gather.9.cloned.1.call-done = bf16[768,768]{1,0:T(8,128)(2,1)} async-done(((bf16[48,768]{1,0:T(8,128)(2,1)}), bf16[768,768]{1,0:T(8,128)(2,1)}) %all-gather.9.cloned.1.call-update) | async-done | bytes 1179664 | tf_op jit(solution)/shard_map/all_gather | solution.py:85
  103.8 50.9 %all-gather.11.cloned.1.call-done = bf16[768,3072]{1,0:T(8,128)(2,1)} async-done(((bf16[48,3072]{1,0:T(8,128)(2,1)}), bf16[768,3072]{1,0:T(8,128)(2,1)}) %all-gather.11.cloned.1.call-update) | async-done | bytes 4718608 | tf_op jit(solution)/shard_map/all_gather | solution.py:86
  160.0 48.6 %all-gather.13.cloned.1.call-done = bf16[768,3072]{1,0:T(8,128)(2,1)} async-done(((bf16[48,3072]{1,0:T(8,128)(2,1)}), bf16[768,3072]{1,0:T(8,128)(2,1)}) %all-gather.13.cloned.1.call-update) | async-done | bytes 4718608 | tf_op jit(solution)/shard_map/all_gather | solution.py:87
  208.6 7.2 multiply_convert_fusion.2
  215.8 46.8 %all-gather.15.cloned.1.call-done = bf16[3072,768]{1,0:T(8,128)(2,1)} async-done(((bf16[192,768]{1,0:T(8,128)(2,1)}), bf16[3072,768]{1,0:T(8,128)(2,1)}) %all-gather.15.cloned.1.call-update) | async-done | bytes 4718608 | tf_op jit(solution)/shard_map/all_gather | solution.py:88
  269.5 40.3 %all-gather = f32[32,4,768]{2,1,0:T(4,128)S(1)} all-gather(f32[1,4,768]{2,1,0:T(4,128)S(1)} %multiply_bitcast_fusion), channel_id=1, replica_groups=mesh['tower'=2,'dp'=16] {'tower','dp'}, dimensions={0}, use_global_device_ids=true | all-gather | bytes 405504 | tf_op jit(solution)/shard_map/all_gather | solution.py:147
  324.4 7.6 multiply_convert_fusion.1
  355.3 8.1 copy.70
  383.5 15.4 %reduce-scatter.15.cloned.1.call-done = f32[48,768]{1,0:T(8,128)} async-done(((f32[768,768]{1,0:T(8,128)}), f32[48,768]{1,0:T(8,128)}) %reduce-scatter.15.cloned.1.call-update) | async-done | bytes 147472 | tf_op jit(solution)/shard_map/reduce_scatter | solution.py:238
  400.5 92.0 %reduce-scatter.31.cloned.1.call-done = f32[48,2304]{1,0:T(8,128)} async-done(((f32[768,2304]{1,0:T(8,128)}), f32[48,2304]{1,0:T(8,128)}) %reduce-scatter.31.cloned.1.call-update) | async-done | bytes 442384
  494.9 112.7 %reduce-scatter.19.cloned.1.call-done = f32[48,3072]{1,0:T(8,128)} async-done(((f32[768,3072]{1,0:T(8,128)}), f32[48,3072]{1,0:T(8,128)}) %reduce-scatter.19.cloned.1.call-update) | async-done | bytes 589840 | tf_op jit(solution)/shard_map/reduce_scatter | solution.py:239
  609.4 113.9 %reduce-scatter.23.cloned.1.call-done = f32[48,3072]{1,0:T(8,128)} async-done(((f32[768,3072]{1,0:T(8,128)}), f32[48,3072]{1,0:T(8,128)}) %reduce-scatter.23.cloned.1.call-update) | async-done | bytes 589840 | tf_op jit(solution)/shard_map/reduce_scatter | solution.py:240
  727.2 62.3 %all-reduce.21 = (bf16[768]{0:T(1024)(128)(2,1)S(1)}, bf16[768]{0:T(1024)(128)(2,1)S(1)}, bf16[768]{0:T(1024)(128)(2,1)S(1)}, bf16[768]{0:T(1024)(128)(2,1)S(1)}) all-reduce(f32[768]{0:T(1024)S(1)} %copy-done.63, f32[768]{0:T(1024)S(1)} %copy-done.64, f32[768]{0:T(1024)S(1)} %copy-done.48, ...), channel_id=12, replica_groups=mesh['tower'=2,'dp'=16] {'dp'}, use_global_device_ids=true, to_apply=%region_29.30.clone | all-reduce | flops 3072 | bytes 18432
  806.4 32.3 %reduce-scatter.27.cloned.1.call-done = f32[192,768]{1,0:T(8,128)} async-done(((f32[3072,768]{1,0:T(8,128)}), f32[192,768]{1,0:T(8,128)}) %reduce-scatter.27.cloned.1.call-update) | async-done | bytes 589840 | tf_op jit(solution)/shard_map/reduce_scatter | solution.py:241
  844.6 6.7 reduce-scatter.17.cloned.1.call-done
  856.8 7.9 reduce-scatter.33.cloned.1.call-done
  864.7 5.7 all_gather.67
  871.1 8.5 reduce-scatter.21.cloned.1.call-done
  879.6 6.5 all_gather.69
  886.9 6.9 reduce-scatter.25.cloned.1.call-done
  893.9 6.5 all_gather.70
  901.2 6.9 reduce-scatter.29.cloned.1.call-done
  908.1 6.5 all_gather.71
  (295 shorter events, 138.7 us)
Async XLA Ops:
  7.2 53.2 %all-gather.7.cloned.1.call-start = ((), (), s32[]{:S(2)}) async-start(), calls=%async_computation.10 | async-start | bytes 3760128 | tf_op jit(solution)/shard_map/all_gather | solution.py:84
  7.9 92.2 %all-gather.9.cloned.1.call-start = ((), (), s32[]{:S(2)}) async-start(), calls=%async_computation.11 | async-start | bytes 1253376 | tf_op jit(solution)/shard_map/all_gather | solution.py:85
  8.7 146.0 %all-gather.11.cloned.1.call-start = ((), (), s32[]{:S(2)}) async-start(), calls=%async_computation.12 | async-start | bytes 5013504 | tf_op jit(solution)/shard_map/all_gather | solution.py:86
  9.4 199.2 %all-gather.13.cloned.1.call-start = ((), (), s32[]{:S(2)}) async-start(), calls=%async_computation.13 | async-start | bytes 5013504 | tf_op jit(solution)/shard_map/all_gather | solution.py:87
  10.0 252.6 %all-gather.15.cloned.1.call-start = ((), (), s32[]{:S(2)}) async-start(), calls=%async_computation.14 | async-start | bytes 5013504 | tf_op jit(solution)/shard_map/all_gather | solution.py:88
  10.6 388.3 %reduce-scatter.15.cloned.1.call-start = ((), (), s32[]{:S(2)}) async-start(), calls=%async_computation.15 | async-start | bytes 2506752 | tf_op jit(solution)/shard_map/reduce_scatter | solution.py:238
  339.4 153.1 %reduce-scatter.31.cloned.1.call-start = ((), (), s32[]{:S(2)}) async-start(), calls=%async_computation.23 | async-start | bytes 7520256
  363.4 244.1 %reduce-scatter.19.cloned.1.call-start = ((), (), s32[]{:S(2)}) async-start(), calls=%async_computation.17 | async-start | bytes 10027008 | tf_op jit(solution)/shard_map/reduce_scatter | solution.py:239
  370.0 353.3 %reduce-scatter.23.cloned.1.call-start = ((), (), s32[]{:S(2)}) async-start(), calls=%async_computation.19 | async-start | bytes 10027008 | tf_op jit(solution)/shard_map/reduce_scatter | solution.py:240
  376.5 462.2 %reduce-scatter.27.cloned.1.call-start = ((), (), s32[]{:S(2)}) async-start(), calls=%async_computation.21 | async-start | bytes 10027008 | tf_op jit(solution)/shard_map/reduce_scatter | solution.py:241
  383.3 343.8 %copy-start.48 = (f32[768]{0:T(1024)S(1)}, f32[768]{0:T(1024)}, u32[]{:S(2)}) copy-start(f32[768]{0:T(1024)} %get-tuple-element.39) | copy-start | bytes 9220
  383.3 343.8 %copy-start.49 = (f32[768]{0:T(1024)S(1)}, f32[768]{0:T(1024)}, u32[]{:S(2)}) copy-start(f32[768]{0:T(1024)} %get-tuple-element.43) | copy-start | bytes 9220
  383.3 343.8 %copy-start.63 = (f32[768]{0:T(1024)S(1)}, f32[768]{0:T(1024)}, u32[]{:S(2)}) copy-start(f32[768]{0:T(1024)} %get-tuple-element.41) | copy-start | bytes 9220
  383.3 343.8 %copy-start.64 = (f32[768]{0:T(1024)S(1)}, f32[768]{0:T(1024)}, u32[]{:S(2)}) copy-start(f32[768]{0:T(1024)} %get-tuple-element.44) | copy-start | bytes 9220
  383.4 457.1 %copy-start.4 = (f32[256,768]{1,0:T(8,128)S(1)}, f32[256,768]{1,0:T(8,128)}, u32[]{:S(2)}) copy-start(f32[256,768]{1,0:T(8,128)} %copy-done.3) | copy-start | bytes 2359300
  383.4 457.1 %copy-start.11 = (bf16[256,12,64]{0,2,1:T(8,128)(2,1)S(1)}, bf16[256,12,64]{0,2,1:T(8,128)(2,1)}, u32[]{:S(2)}) copy-start(bf16[256,12,64]{0,2,1:T(8,128)(2,1)} %copy-done.10) | copy-start | bytes 1179652
  383.4 457.1 %copy-start.13 = (bf16[256,12,64]{0,2,1:T(8,128)(2,1)S(1)}, bf16[256,12,64]{0,2,1:T(8,128)(2,1)}, u32[]{:S(2)}) copy-start(bf16[256,12,64]{0,2,1:T(8,128)(2,1)} %copy-done.12) | copy-start | bytes 1179652
  383.4 457.1 %copy-start.33 = (bf16[12,64,256]{2,1,0:T(8,128)(2,1)S(1)}, bf16[12,64,256]{2,1,0:T(8,128)(2,1)}, u32[]{:S(2)}) copy-start(bf16[12,64,256]{2,1,0:T(8,128)(2,1)} %copy-done.32) | copy-start | bytes 1179652
  383.4 457.1 %copy-start.57 = (f32[256]{0:T(256)S(1)}, f32[256]{0:T(256)}, u32[]{:S(2)}) copy-start(f32[256]{0:T(256)} %copy-done.56) | copy-start | bytes 3076
  383.4 467.8 %reduce-scatter.17.cloned.1.call-start = ((), (), s32[]{:S(2)}) async-start(), calls=%async_computation.16 | async-start | bytes 110592 | tf_op jit(solution)/shard_map/reduce_scatter | solution.py:251
  400.4 464.2 %reduce-scatter.33.cloned.1.call-start = ((), (), s32[]{:S(2)}) async-start(), calls=%async_computation.24 | async-start | bytes 331776 | tf_op jit(solution)/shard_map/reduce_scatter | solution.py:248
  494.8 384.8 %reduce-scatter.21.cloned.1.call-start = ((), (), s32[]{:S(2)}) async-start(), calls=%async_computation.18 | async-start | bytes 442368 | tf_op jit(solution)/shard_map/reduce_scatter | solution.py:254
  609.4 284.5 %reduce-scatter.25.cloned.1.call-start = ((), (), s32[]{:S(2)}) async-start(), calls=%async_computation.20 | async-start | bytes 442368 | tf_op jit(solution)/shard_map/reduce_scatter | solution.py:257
  725.2 182.9 %reduce-scatter.29.cloned.1.call-start = ((), (), s32[]{:S(2)}) async-start(), calls=%async_computation.22 | async-start | bytes 442368 | tf_op jit(solution)/shard_map/reduce_scatter | solution.py:260
  (64 other events, 344.3 us)
Sparse Core Ops, SparseCore 0:
  10.3 50.0 all-gather.6
  62.7 37.4 all-gather.8
  102.4 52.1 all-gather.10
  156.8 51.7 all-gather.12
  210.7 51.7 all-gather.14
  339.5 59.2 reduce-scatter.14
  403.4 89.0 reduce-scatter.30
  496.6 110.8 reduce-scatter.18
  612.2 111.1 reduce-scatter.22
  727.3 111.3 reduce-scatter.26
  841.5 9.6 reduce-scatter.16
  853.4 11.1 reduce-scatter.32
  867.6 12.0 reduce-scatter.20
  881.8 12.0 reduce-scatter.24
  896.0 12.0 reduce-scatter.28
where the time goes:
time: 924 us; the launch traced here: 923 us
  waiting for transfers between devices  585 us (63%)
  blocking collectives  178 us (19%)
  matrix products  75.5 us (8%)
  local copies, waits for them, and re-layouts  37.5 us (4%)
  other arithmetic  26.3 us (3%)
  between operations  20 us (2%)
    reduce_scatter x1, waiting for transfers between devices, on_device(): lax.psum_scatter(gradients[3], 'dp', scatter_dimension=0, tiled=True)  114 us
    reduce_scatter x1, waiting for transfers between devices, on_device(): lax.psum_scatter(gradients[2], 'dp', scatter_dimension=0, tiled=True)  113 us
    unnamed x4, blocking collectives  108 us
    unnamed x16, waiting for transfers between devices  95.3 us
    dot_general x15, matrix products, product(): return jnp.dot(left, right, preferred_element_type=jnp.float32)  61.8 us
    all_gather x1, waiting for transfers between devices, on_device(): lax.all_gather(w_gate, 'dp', axis=0, tiled=True)  50.9 us
    all_gather x1, waiting for transfers between devices, on_device(): lax.all_gather(w_up, 'dp', axis=0, tiled=True)  48.6 us
    all_gather x1, waiting for transfers between devices, on_device(): lax.all_gather(w_down, 'dp', axis=0, tiled=True)  46.8 us
  transfers between devices with their start and end apart: 15, of which 15 were waited for; matrix products, arithmetic and copies ran while one was open for 10% of the time, Pallas kernels for 0%

commit v1 on v0

--- a/solution.py
+++ b/solution.py
@@ -11,6 +11,28 @@
 exact_product_accuracy = lax.Precision.HIGHEST
 rope_base = 1000.0
 contrast_sharpness_factor = 0.02
+
+
+def laid_out(pieces, dim):
+    lengths = list(pieces.shape[1:])
+    lengths[dim] *= pieces.shape[0]
+    return jnp.moveaxis(pieces, 0, dim).reshape(lengths)
+
+
+def gather_around(x, axis, dim):
+    size = lax.axis_size(axis)
+    pairs = [(i, (i + 1) % size) for i in range(size)]
+    back = [(b, a) for a, b in pairs]
+    lower, upper = ([], [])
+    for lap in range(size - 1):
+        if lap % 2 == 0:
+            lower.append(lax.ppermute(lower[-1] if lower else x, axis, pairs))
+        else:
+            upper.append(lax.ppermute(upper[-1] if upper else x, axis, back))
+    parts = jnp.stack([*lower[::-1], x, *upper])
+    shift = lax.axis_index(axis) - len(lower)
+    parts = parts[(jnp.arange(size) - shift) % size]
+    return laid_out(parts, dim)
 
 
 def product(left, right):
@@ -83,7 +105,7 @@
     full = (
         lax.all_gather(w_qkv, "dp", axis=0, tiled=True),
         lax.all_gather(w_out, "dp", axis=0, tiled=True),
-        lax.all_gather(w_gate, "dp", axis=0, tiled=True),
+        gather_around(w_gate, "dp", 0),
         lax.all_gather(w_up, "dp", axis=0, tiled=True),
         lax.all_gather(w_down, "dp", axis=0, tiled=True),
         lax.all_gather(ln1_gain, "dp", axis=0, tiled=True),

time: 924 us -> 883 us (0.956)
  waiting for transfers between devices: 585 us -> 497 us
  starting transfers between devices: 0.82 us -> 29.4 us
  local copies, waits for them, and re-layouts: 37.5 us -> 54.9 us
    all_gather x1 -> x0, waiting for transfers between devices: 50.9 us -> none  [on_device(): lax.all_gather(w_gate, 'dp', axis=0, tiled=True)]
    all_gather x1, waiting for transfers between devices: 48.6 us -> 5.59 us  [on_device(): lax.all_gather(w_up, 'dp', axis=0, tiled=True)]
    ppermute x0 -> x15, waiting for transfers between devices: none -> 37.7 us  [the longest x8 23.9 us: gather_around(): lower.append(lax.ppermute(lower[-1] if lower else x, axis, pairs))]
    ppermute x0 -> x15, starting transfers between devices: none -> 28.6 us  [the longest x7 27.5 us: gather_around(): upper.append(lax.ppermute(upper[-1] if upper else x, axis, back))]
    all_gather x1, waiting for transfers between devices: 28.5 us -> 0.01 us  [on_device(): lax.all_gather(w_out, 'dp', axis=0, tiled=True)]
    unnamed x174 -> x189, local copies, waits for them, and re-layouts: 26.4 us -> 37.6 us
    unnamed x16 -> x15, waiting for transfers between devices: 95.3 us -> 94.2 us
  transfers between devices with their start and end apart: 15 -> 29, of which waited for: 15 -> 23; matrix products, arithmetic and copies ran while one was open for 10% -> 13% of each run, Pallas kernels for 0% -> 0%
where the time goes in v1:
time: 883 us; the launch traced here: 882 us
  waiting for transfers between devices  497 us (56%)
  blocking collectives  178 us (20%)
  matrix products  76.4 us (9%)
  local copies, waits for them, and re-layouts  54.9 us (6%)
  starting transfers between devices  29.4 us (3%)
  other arithmetic  26.8 us (3%)
  between operations  20 us (2%)
    reduce_scatter x1, waiting for transfers between devices, on_device(): lax.psum_scatter(gradients[3], 'dp', scatter_dimension=0, tiled=True)  114 us
    reduce_scatter x1, waiting for transfers between devices, on_device(): lax.psum_scatter(gradients[2], 'dp', scatter_dimension=0, tiled=True)  113 us
    unnamed x4, blocking collectives  107 us
    unnamed x15, waiting for transfers between devices  94.2 us
    dot_general x15, matrix products, product(): return jnp.dot(left, right, preferred_element_type=jnp.float32)  61.8 us
    all_gather x1, waiting for transfers between devices, on_device(): lax.all_gather(w_down, 'dp', axis=0, tiled=True)  46.9 us
    all_gather x1, blocking collectives, on_device(): gathered = lax.all_gather(embedded, ('tower', 'dp'), axis=0, tiled=True)  40.3 us
    unnamed x189, local copies, waits for them, and re-layouts  37.6 us
  transfers between devices with their start and end apart: 29, of which 23 were waited for; matrix products, arithmetic and copies ran while one was open for 13% of the time, Pallas kernels for 0%

profile of v1, /device:TPU:0, one launch (start us, length us, event | category | flops | bytes accessed | tf_op | source)
XLA Modules:
  0.0 881.9 jit_solution(12851647384505985561)
XLA Ops:
  10.0 9.6 %collective-permute-done = bf16[48,3072]{1,0:T(8,128)(2,1)S(1)} collective-permute-done((bf16[48,3072]{1,0:T(8,128)(2,1)}, bf16[48,3072]{1,0:T(8,128)(2,1)S(1)}, u32[]{:S(2)}, u32[]{:S(2)}) %collective-permute-start) | collective-permute-done | bytes 294944 | tf_op jit(solution)/shard_map/ppermute | solution.py:29
  24.0 8.0 collective-permute-done.1
  46.9 34.9 %all-reduce.22 = (bf16[768]{0:T(1024)(128)(2,1)S(1)}, bf16[768]{0:T(1024)(128)(2,1)S(1)}, bf16[768]{0:T(1024)(128)(2,1)S(1)}, bf16[768]{0:T(1024)(128)(2,1)S(1)}) all-reduce(bf16[768]{0:T(1024)(128)(2,1)S(1)} %dynamic-update-slice.1, bf16[768]{0:T(1024)(128)(2,1)S(1)} %dynamic-update-slice, ...), channel_id=1, replica_groups=mesh['tower'=2,'dp'=16] {'dp'}, use_global_device_ids=true, to_apply=%add.6 | all-reduce | flops 3072 | bytes 12288
  160.4 5.6 all-gather.10.cloned.1.call-done
  166.0 7.1 multiply_convert_fusion.2
  173.2 46.9 %all-gather.12.cloned.1.call-done = bf16[3072,768]{1,0:T(8,128)(2,1)} async-done(((bf16[192,768]{1,0:T(8,128)(2,1)}), bf16[3072,768]{1,0:T(8,128)(2,1)}) %all-gather.12.cloned.1.call-update) | async-done | bytes 4718608 | tf_op jit(solution)/shard_map/all_gather | solution.py:110
  227.0 40.3 %all-gather = f32[32,4,768]{2,1,0:T(4,128)S(1)} all-gather(f32[1,4,768]{2,1,0:T(4,128)S(1)} %multiply_bitcast_fusion), channel_id=1, replica_groups=mesh['tower'=2,'dp'=16] {'tower','dp'}, dimensions={0}, use_global_device_ids=true | all-gather | bytes 405504 | tf_op jit(solution)/shard_map/all_gather | solution.py:169
  282.0 7.6 multiply_convert_fusion.1
  312.9 8.0 copy.70
  341.1 15.4 %reduce-scatter.15.cloned.1.call-done = f32[48,768]{1,0:T(8,128)} async-done(((f32[768,768]{1,0:T(8,128)}), f32[48,768]{1,0:T(8,128)}) %reduce-scatter.15.cloned.1.call-update) | async-done | bytes 147472 | tf_op jit(solution)/shard_map/reduce_scatter | solution.py:260
  358.1 91.9 %reduce-scatter.31.cloned.1.call-done = f32[48,2304]{1,0:T(8,128)} async-done(((f32[768,2304]{1,0:T(8,128)}), f32[48,2304]{1,0:T(8,128)}) %reduce-scatter.31.cloned.1.call-update) | async-done | bytes 442384
  452.3 112.7 %reduce-scatter.19.cloned.1.call-done = f32[48,3072]{1,0:T(8,128)} async-done(((f32[768,3072]{1,0:T(8,128)}), f32[48,3072]{1,0:T(8,128)}) %reduce-scatter.19.cloned.1.call-update) | async-done | bytes 589840 | tf_op jit(solution)/shard_map/reduce_scatter | solution.py:261
  566.9 113.9 %reduce-scatter.23.cloned.1.call-done = f32[48,3072]{1,0:T(8,128)} async-done(((f32[768,3072]{1,0:T(8,128)}), f32[48,3072]{1,0:T(8,128)}) %reduce-scatter.23.cloned.1.call-update) | async-done | bytes 589840 | tf_op jit(solution)/shard_map/reduce_scatter | solution.py:262
  684.7 62.3 %all-reduce.21 = (bf16[768]{0:T(1024)(128)(2,1)S(1)}, bf16[768]{0:T(1024)(128)(2,1)S(1)}, bf16[768]{0:T(1024)(128)(2,1)S(1)}, bf16[768]{0:T(1024)(128)(2,1)S(1)}) all-reduce(f32[768]{0:T(1024)S(1)} %copy-done.63, f32[768]{0:T(1024)S(1)} %copy-done.64, f32[768]{0:T(1024)S(1)} %copy-done.48, ...), channel_id=12, replica_groups=mesh['tower'=2,'dp'=16] {'dp'}, use_global_device_ids=true, to_apply=%region_29.30.clone | all-reduce | flops 3072 | bytes 18432
  763.9 33.6 %reduce-scatter.27.cloned.1.call-done = f32[192,768]{1,0:T(8,128)} async-done(((f32[3072,768]{1,0:T(8,128)}), f32[192,768]{1,0:T(8,128)}) %reduce-scatter.27.cloned.1.call-update) | async-done | bytes 589840 | tf_op jit(solution)/shard_map/reduce_scatter | solution.py:263
  803.4 6.5 reduce-scatter.17.cloned.1.call-done
  815.5 8.1 reduce-scatter.33.cloned.1.call-done
  823.5 5.7 all_gather.63
  830.0 8.4 reduce-scatter.21.cloned.1.call-done
  838.4 6.4 all_gather.65
  845.7 7.1 reduce-scatter.25.cloned.1.call-done
  852.7 6.4 all_gather.66
  860.0 6.9 reduce-scatter.29.cloned.1.call-done
  867.0 6.4 all_gather.67
  (341 shorter events, 202.0 us)
Async XLA Ops:
  7.2 132.5 %all-gather.6.cloned.1.call-start = ((), (), s32[]{:S(2)}) async-start(), calls=%async_computation.10 | async-start | bytes 3760128 | tf_op jit(solution)/shard_map/all_gather | solution.py:106
  7.9 143.5 %all-gather.8.cloned.1.call-start = ((), (), s32[]{:S(2)}) async-start(), calls=%async_computation.11 | async-start | bytes 1253376 | tf_op jit(solution)/shard_map/all_gather | solution.py:107
  8.7 157.4 %all-gather.10.cloned.1.call-start = ((), (), s32[]{:S(2)}) async-start(), calls=%async_computation.12 | async-start | bytes 5013504 | tf_op jit(solution)/shard_map/all_gather | solution.py:109
  9.4 210.6 %all-gather.12.cloned.1.call-start = ((), (), s32[]{:S(2)}) async-start(), calls=%async_computation.13 | async-start | bytes 5013504 | tf_op jit(solution)/shard_map/all_gather | solution.py:110
  9.5 10.1 %collective-permute-start = (bf16[48,3072]{1,0:T(8,128)(2,1)}, bf16[48,3072]{1,0:T(8,128)(2,1)S(1)}, u32[]{:S(2)}, u32[]{:S(2)}) collective-permute-start(bf16[48,3072]{1,0:T(8,128)(2,1)} %param.19), channel_id=1, source_target_pairs={{0,1},{1,2},{2,3},{3,4},{4,5},{5,6},{6,7},{7,8},{8,9},{9,10},{10,1... | collective-permute-start | bytes 884744 | tf_op jit(solution)/shard_map/ppermute | solution.py:29
  19.5 12.5 %collective-permute-start.1 = (bf16[48,3072]{1,0:T(8,128)(2,1)S(1)}, bf16[48,3072]{1,0:T(8,128)(2,1)S(1)}, u32[]{:S(2)}, u32[]{:S(2)}) collective-permute-start(bf16[48,3072]{1,0:T(8,128)(2,1)S(1)} %collective-permute-done), channel_id=1, source_target_pairs={{0,1},{1,2},{2,3},{3,4},{4,5},{5,6},{6,7},{7,8},{8,9},{9,10},{10,1... | collective-permute-start | bytes 884744 | tf_op jit(solution)/shard_map/ppermute | solution.py:29
  19.5 12.5 %collective-permute-start.8 = (bf16[48,3072]{1,0:T(8,128)(2,1)}, bf16[48,3072]{1,0:T(8,128)(2,1)S(1)}, u32[]{:S(2)}, u32[]{:S(2)}) collective-permute-start(bf16[48,3072]{1,0:T(8,128)(2,1)} %param.19), channel_id=1, source_target_pairs={{1,0},{2,1},{3,2},{4,3},{5,4},{6,5},{7,6},{8,7},{9,8},{10,9},{11,1... | collective-permute-start | bytes 884744 | tf_op jit(solution)/shard_map/ppermute | solution.py:31
  32.0 52.5 %collective-permute-start.9 = (bf16[48,3072]{1,0:T(8,128)(2,1)S(1)}, bf16[48,3072]{1,0:T(8,128)(2,1)S(1)}, u32[]{:S(2)}, u32[]{:S(2)}) collective-permute-start(bf16[48,3072]{1,0:T(8,128)(2,1)S(1)} %collective-permute-done.8), channel_id=1, source_target_pairs={{1,0},{2,1},{3,2},{4,3},{5,4},{6,5},{7,6},{8,7},{9,8},{10,9},{11,1... | collective-permute-start | bytes 884744 | tf_op jit(solution)/shard_map/ppermute | solution.py:31
  40.8 43.8 %collective-permute-start.3 = (bf16[48,3072]{1,0:T(8,128)(2,1)S(1)}, bf16[48,3072]{1,0:T(8,128)(2,1)S(1)}, u32[]{:S(2)}, u32[]{:S(2)}) collective-permute-start(bf16[48,3072]{1,0:T(8,128)(2,1)S(1)} %collective-permute-done.2), channel_id=1, source_target_pairs={{0,1},{1,2},{2,3},{3,4},{4,5},{5,6},{6,7},{7,8},{8,9},{9,10},{10,1... | collective-permute-start | bytes 884744 | tf_op jit(solution)/shard_map/ppermute | solution.py:29
  40.9 315.6 %reduce-scatter.15.cloned.1.call-start = ((), (), s32[]{:S(2)}) async-start(), calls=%async_computation.14 | async-start | bytes 2506752 | tf_op jit(solution)/shard_map/reduce_scatter | solution.py:260
  84.6 9.0 %collective-permute-start.4 = (bf16[48,3072]{1,0:T(8,128)(2,1)S(1)}, bf16[48,3072]{1,0:T(8,128)(2,1)S(1)}, u32[]{:S(2)}, u32[]{:S(2)}) collective-permute-start(bf16[48,3072]{1,0:T(8,128)(2,1)S(1)} %collective-permute-done.3), channel_id=1, source_target_pairs={{0,1},{1,2},{2,3},{3,4},{4,5},{5,6},{6,7},{7,8},{8,9},{9,10},{10,1... | collective-permute-start | bytes 884744 | tf_op jit(solution)/shard_map/ppermute | solution.py:29
  88.8 10.4 %collective-permute-start.11 = (bf16[48,3072]{1,0:T(8,128)(2,1)S(1)}, bf16[48,3072]{1,0:T(8,128)(2,1)S(1)}, u32[]{:S(2)}, u32[]{:S(2)}) collective-permute-start(bf16[48,3072]{1,0:T(8,128)(2,1)S(1)} %collective-permute-done.10), channel_id=1, source_target_pairs={{1,0},{2,1},{3,2},{4,3},{5,4},{6,5},{7,6},{8,7},{9,8},{10,9},{11,1... | collective-permute-start | bytes 884744 | tf_op jit(solution)/shard_map/ppermute | solution.py:31
  93.6 10.9 %collective-permute-start.5 = (bf16[48,3072]{1,0:T(8,128)(2,1)S(1)}, bf16[48,3072]{1,0:T(8,128)(2,1)S(1)}, u32[]{:S(2)}, u32[]{:S(2)}) collective-permute-start(bf16[48,3072]{1,0:T(8,128)(2,1)S(1)} %collective-permute-done.4), channel_id=1, source_target_pairs={{0,1},{1,2},{2,3},{3,4},{4,5},{5,6},{6,7},{7,8},{8,9},{9,10},{10,1... | collective-permute-start | bytes 884744 | tf_op jit(solution)/shard_map/ppermute | solution.py:29
  113.4 9.0 %collective-permute-start.7 = (bf16[48,3072]{1,0:T(8,128)(2,1)S(1)}, bf16[48,3072]{1,0:T(8,128)(2,1)S(1)}, u32[]{:S(2)}, u32[]{:S(2)}) collective-permute-start(bf16[48,3072]{1,0:T(8,128)(2,1)S(1)} %collective-permute-done.6), channel_id=1, source_target_pairs={{0,1},{1,2},{2,3},{3,4},{4,5},{5,6},{6,7},{7,8},{8,9},{9,10},{10,1... | collective-permute-start | bytes 884744 | tf_op jit(solution)/shard_map/ppermute | solution.py:29
  117.1 16.4 %collective-permute-start.14 = (bf16[48,3072]{1,0:T(8,128)(2,1)S(1)}, bf16[48,3072]{1,0:T(8,128)(2,1)S(1)}, u32[]{:S(2)}, u32[]{:S(2)}) collective-permute-start(bf16[48,3072]{1,0:T(8,128)(2,1)S(1)} %collective-permute-done.13), channel_id=1, source_target_pairs={{1,0},{2,1},{3,2},{4,3},{5,4},{6,5},{7,6},{8,7},{9,8},{10,9},{11,1... | collective-permute-start | bytes 884744 | tf_op jit(solution)/shard_map/ppermute | solution.py:31
  297.1 153.0 %reduce-scatter.31.cloned.1.call-start = ((), (), s32[]{:S(2)}) async-start(), calls=%async_computation.22 | async-start | bytes 7520256
  321.0 244.1 %reduce-scatter.19.cloned.1.call-start = ((), (), s32[]{:S(2)}) async-start(), calls=%async_computation.16 | async-start | bytes 10027008 | tf_op jit(solution)/shard_map/reduce_scatter | solution.py:261
  327.7 353.2 %reduce-scatter.23.cloned.1.call-start = ((), (), s32[]{:S(2)}) async-start(), calls=%async_computation.18 | async-start | bytes 10027008 | tf_op jit(solution)/shard_map/reduce_scatter | solution.py:262
  334.1 463.4 %reduce-scatter.27.cloned.1.call-start = ((), (), s32[]{:S(2)}) async-start(), calls=%async_computation.20 | async-start | bytes 10027008 | tf_op jit(solution)/shard_map/reduce_scatter | solution.py:263
  341.1 468.9 %reduce-scatter.17.cloned.1.call-start = ((), (), s32[]{:S(2)}) async-start(), calls=%async_computation.15 | async-start | bytes 110592 | tf_op jit(solution)/shard_map/reduce_scatter | solution.py:273
  358.0 465.5 %reduce-scatter.33.cloned.1.call-start = ((), (), s32[]{:S(2)}) async-start(), calls=%async_computation.23 | async-start | bytes 331776 | tf_op jit(solution)/shard_map/reduce_scatter | solution.py:270
  452.3 386.1 %reduce-scatter.21.cloned.1.call-start = ((), (), s32[]{:S(2)}) async-start(), calls=%async_computation.17 | async-start | bytes 442368 | tf_op jit(solution)/shard_map/reduce_scatter | solution.py:276
  566.9 285.9 %reduce-scatter.25.cloned.1.call-start = ((), (), s32[]{:S(2)}) async-start(), calls=%async_computation.19 | async-start | bytes 442368 | tf_op jit(solution)/shard_map/reduce_scatter | solution.py:279
  682.7 184.3 %reduce-scatter.29.cloned.1.call-start = ((), (), s32[]{:S(2)}) async-start(), calls=%async_computation.21 | async-start | bytes 442368 | tf_op jit(solution)/shard_map/reduce_scatter | solution.py:282
  (78 other events, 4171.1 us)
Sparse Core Ops, SparseCore 0:
  10.3 54.1 all-gather.5
  66.8 42.1 all-gather.7
  111.3 54.7 all-gather.9
  168.2 51.8 all-gather.11
  297.2 59.2 reduce-scatter.14
  360.9 89.1 reduce-scatter.30
  454.1 110.8 reduce-scatter.18
  569.7 111.1 reduce-scatter.22
  684.9 112.5 reduce-scatter.26
  800.2 9.6 reduce-scatter.16
  812.3 11.2 reduce-scatter.32
  826.3 12.0 reduce-scatter.20
  840.7 12.0 reduce-scatter.24
  854.9 12.0 reduce-scatter.28
